TPU v7x, 256 devices: a whole 4x4x8 slice. The times are simulated.
256 devices in a mesh: lat: 4 (over x_lo, core), lon: 64 (over x_hi, y, z).
Axes of the slice: x: 4 (x_hi: 2, x_lo: 2; x = x_hi * 2 + x_lo), y: 4, z: 8, core: 2. Of those that a mesh axis runs over, the one named last changes fastest.
Arguments:
- queries: bfloat16 [64, 1024, 1536], P('lat', 'lon'), may hold values from -12 to 12
- key_tokens: bfloat16 [64, 1024, 1536], P('lat', 'lon'), may hold values from -4 to 4
- value_tokens: bfloat16 [64, 1024, 1536], P('lat', 'lon'), may hold values from -6 to 6
- block_lists: int32 [8, 64, 8], P('lat', 'lon'), may hold values from 0 to 9, as said below
- band_rows: int32 [4, 1024], P('lat', 'lon'), may hold values from 0 to 255, as said below
Outputs:
- attended: bfloat16 [64, 1024, 1536], P('lat', 'lon')
Inputs may be any that keep to these rules, and one draw needn't show every extreme that they name: `block_lists`: entry 0 of the list of query block b of a tile is its own block, 4 + b; the other entries are distinct candidate numbers, also distinct from entry 0. `band_rows`: the 16 token numbers of each tile are distinct.
All inputs are finite; a program needn't handle non-finite values.
Results may differ from a plain program's by a relative error of at most 0.0047.
Values may be sent and summed in bfloat16 or wider, within the bound.
No kernel may reach another device: no remote copies, remote signals or barrier semaphores. Data moves between devices by JAX's collectives and lax.ppermute only.
A program may use at most 128 MiB of HBM per device.

v0:
```python
import jax
import jax.numpy as jnp
from jax import lax
from jax.sharding import PartitionSpec as P

H = 24
HD = 64
BR = 8
BW = 16


def from_behind(value, axis, steps):
    count = lax.axis_size(axis)
    pairs = [(source, (source + steps) % count) for source in range(count)]
    return lax.ppermute(value, axis, pairs)


def block_attention(q_rows, key_set, value_set, live_mask):
    count = q_rows.shape[0]
    q_heads = q_rows.reshape(count, H, HD)
    k_heads = key_set.reshape(key_set.shape[0], H, HD)
    v_heads = value_set.reshape(value_set.shape[0], H, HD)
    scores = jnp.einsum(
        "qhd,khd->hqk", q_heads, k_heads, preferred_element_type=jnp.float32
    ) * HD ** (-0.5)
    scores = jnp.where(live_mask[None, None, :], scores, -jnp.inf)
    row_max = jnp.max(scores, axis=-1, keepdims=True)
    exp_scores = jnp.exp(scores - row_max)
    totals = jnp.sum(exp_scores, axis=-1)
    weights = exp_scores.astype(jnp.bfloat16)
    mixture = jnp.einsum("hqk,khd->qhd", weights, v_heads, preferred_element_type=jnp.float32)
    mixture = mixture / jnp.transpose(totals)[:, :, None]
    return mixture.reshape(count, H * HD).astype(jnp.bfloat16)


def local(queries, key_tokens, value_tokens, block_lists, band_rows):
    tile_lat, tile_lon, feature = queries.shape
    block_len = BR * BW
    tile_blocks = tile_lat // BR
    lat_size = lax.axis_size("lat")
    west_two = from_behind((key_tokens, value_tokens), "lon", 2)
    west_one = from_behind((key_tokens, value_tokens), "lon", 1)
    east_one = from_behind((key_tokens, value_tokens), "lon", -1)
    east_two = from_behind((key_tokens, value_tokens), "lon", -2)
    sources = (west_two, west_one, (key_tokens, value_tokens), east_one, east_two)
    cand_keys = jnp.concatenate(
        [entry[0].reshape(tile_blocks, block_len, feature) for entry in sources], 0
    )
    cand_values = jnp.concatenate(
        [entry[1].reshape(tile_blocks, block_len, feature) for entry in sources], 0
    )
    picked_keys = key_tokens.reshape(tile_lat * tile_lon, feature)[band_rows[0]]
    picked_values = value_tokens.reshape(tile_lat * tile_lon, feature)[band_rows[0]]
    band_keys, band_values = (
        lax.all_gather(picked_keys, "lon", axis=0, tiled=True),
        lax.all_gather(picked_values, "lon", axis=0, tiled=True),
    )
    lat_at = lax.axis_index("lat")
    is_polar = (lat_at == 0) | (lat_at == lat_size - 1)
    listed_all = block_lists[:, 0, :]
    band_live = jnp.ones((band_keys.shape[0],), jnp.bool_)
    query_blocks = queries.reshape(tile_blocks, block_len, feature)

    def one_block(inputs):
        q_rows, listed = inputs
        near_keys = cand_keys[listed].reshape(-1, feature)
        near_values = cand_values[listed].reshape(-1, feature)
        near_live = jnp.ones((near_keys.shape[0],), jnp.bool_)

        def with_band():
            key_set = jnp.concatenate([near_keys, band_keys], 0)
            value_set = jnp.concatenate([near_values, band_values], 0)
            live_mask = jnp.concatenate([near_live, band_live], 0)
            return block_attention(q_rows, key_set, value_set, live_mask)

        def near_only():
            return block_attention(q_rows, near_keys, near_values, near_live)

        return lax.cond(is_polar, with_band, near_only)

    results = lax.map(one_block, (query_blocks, listed_all))
    return results.reshape(tile_lat, tile_lon, feature)


def solution(mesh):
    return jax.shard_map(
        local,
        mesh=mesh,
        in_specs=(
            P("lat", "lon", None),
            P("lat", "lon", None),
            P("lat", "lon", None),
            P("lat", "lon", None),
            P("lat", "lon"),
        ),
        out_specs=P("lat", "lon", None),
        check_vma=False,
    )
```

profile of v0, /device:TPU:8, one launch (start us, length us, event | category | flops | bytes accessed | tf_op | source)
XLA Modules:
  0.0 465.4 jit_solution(9054206073713176776)
XLA Ops:
  24.4 20.5 %collective-permute-done.4 = bf16[16,16,1536]{2,1,0:T(8,128)(2,1)} collective-permute-done((bf16[16,16,1536]{2,1,0:T(8,128)(2,1)}, bf16[16,16,1536]{2,1,0:T(8,128)(2,1)}, u32[]{:S(2)}, u32[]{:S(2)}) %collective-permute-start.4) | collective-permute-done | bytes 786464 | tf_op jit(solution)/shard_map/ppermute | solution.py:15
  44.9 28.6 %collective-permute-start.6 = (bf16[16,16,1536]{2,1,0:T(8,128)(2,1)}, bf16[16,16,1536]{2,1,0:T(8,128)(2,1)S(1)}, u32[]{:S(2)}, u32[]{:S(2)}) collective-permute-start(bf16[16,16,1536]{2,1,0:T(8,128)(2,1)} %param.11), channel_id=1, source_target_pairs={{0,63},{1,0},{2,1},{3,2},{4,3},{5,4},{6,5},{7,6},{8,7},{9,8},{10,9... | collective-permute-start | bytes 2359304 | tf_op jit(solution)/shard_map/ppermute | solution.py:15
  75.6 5.3 %collective-permute-done = bf16[16,16,1536]{2,1,0:T(8,128)(2,1)} collective-permute-done((bf16[16,16,1536]{2,1,0:T(8,128)(2,1)}, bf16[16,16,1536]{2,1,0:T(8,128)(2,1)}, u32[]{:S(2)}, u32[]{:S(2)}) %collective-permute-start) | collective-permute-done | bytes 786464 | tf_op jit(solution)/shard_map/ppermute | solution.py:15
  80.9 12.4 %collective-permute-start.7 = (bf16[16,16,1536]{2,1,0:T(8,128)(2,1)}, bf16[16,16,1536]{2,1,0:T(8,128)(2,1)S(1)}, u32[]{:S(2)}, u32[]{:S(2)}) collective-permute-start(bf16[16,16,1536]{2,1,0:T(8,128)(2,1)} %param.11), channel_id=1, source_target_pairs={{0,62},{1,63},{2,0},{3,1},{4,2},{5,3},{6,4},{7,5},{8,6},{9,7},{10,... | collective-permute-start | bytes 2359304 | tf_op jit(solution)/shard_map/ppermute | solution.py:15
  95.5 12.5 %collective-permute-done.5 = bf16[16,16,1536]{2,1,0:T(8,128)(2,1)} collective-permute-done((bf16[16,16,1536]{2,1,0:T(8,128)(2,1)}, bf16[16,16,1536]{2,1,0:T(8,128)(2,1)}, u32[]{:S(2)}, u32[]{:S(2)}) %collective-permute-start.5) | collective-permute-done | bytes 786464 | tf_op jit(solution)/shard_map/ppermute | solution.py:15
  114.8 33.9 %collective-permute-done.7 = bf16[16,16,1536]{2,1,0:T(8,128)(2,1)S(1)} collective-permute-done((bf16[16,16,1536]{2,1,0:T(8,128)(2,1)}, bf16[16,16,1536]{2,1,0:T(8,128)(2,1)S(1)}, u32[]{:S(2)}, u32[]{:S(2)}) %collective-permute-start.7) | collective-permute-done | bytes 786464 | tf_op jit(solution)/shard_map/ppermute | solution.py:15
  152.5 14.9 %collective-permute-done.3 = bf16[16,16,1536]{2,1,0:T(8,128)(2,1)S(1)} collective-permute-done((bf16[16,16,1536]{2,1,0:T(8,128)(2,1)S(1)}, bf16[16,16,1536]{2,1,0:T(8,128)(2,1)S(1)}, u32[]{:S(2)}, u32[]{:S(2)}) %collective-permute-start.3) | collective-permute-done | bytes 786464 | tf_op jit(solution)/shard_map/ppermute | solution.py:15
  168.3 26.5 %all-gather.7.cloned.1.call-done = bf16[1024,1536]{1,0:T(8,128)(2,1)} async-done(((bf16[16,1536]{1,0:T(8,128)(2,1)}), bf16[1024,1536]{1,0:T(8,128)(2,1)}) %all-gather.7.cloned.1.call-update) | async-done | bytes 3145744 | tf_op jit(solution)/shard_map/all_gather | solution.py:55
  199.5 121.2 %all-gather.5.cloned.1.call-done = bf16[1024,1536]{1,0:T(8,128)(2,1)} async-done(((bf16[16,1536]{1,0:T(8,128)(2,1)}), bf16[1024,1536]{1,0:T(8,128)(2,1)}) %all-gather.5.cloned.1.call-update) | async-done | bytes 3145744 | tf_op jit(solution)/shard_map/all_gather | solution.py:56
  325.4 133.2 %while.10 = (s32[]{:T(128)}, bf16[2,128,1536]{2,1,0:T(8,128)(2,1)}, pred[]{:T(512)}, bf16[2,128,1536]{2,1,0:T(8,128)(2,1)}, s32[2,8]{1,0:T(2,128)S(1)}, /*index=...) while((s32[]{:T(128)}, bf16[2,128,1536]{2,1,0:T(8,128)(2,1)}, ...), condition=%wide.region_7.8_spmd, body=%wide.region_0.7_spmd.sunk | while | flops 1686498304 | bytes 169148896 | solution.py:81
  334.1 55.2 %conditional.7 = (bf16[1,128,1536]{1,2,0:T(8,128)(2,1)S(1)}) conditional(s32[]{:T(128)} %convert_element_type.36, (bf16[128,1536]{0,1:T(8,128)(2,1)S(1)}, bf16[8,128,1536]{2,1,0:T(8,128)(2,1)}, bf16[8,128,1536]{2,1,0:T(8,128)(2,1)S(1)}) %tuple.53, (bf16[8,128,1536]{2,1,0:T(8,128)(2,1)S(1)}, bf16[1024,1536]{0,1:T(8,128)(2,1)}, ...), branch_computations={%region_1.3_spmd, %region_4.6_spmd} | conditional | flops 1686497280 | bytes 151842912
  334.1 5.0 %copy.14 = bf16[8,128,1536]{1,0,2:T(8,128)(2,1)} copy(bf16[8,128,1536]{2,1,0:T(8,128)(2,1)} %get-tuple-element.102) | data formatting | bytes 6291456 | tf_op jit(solution)/shard_map
  339.1 5.8 %concatenate.17 = bf16[1024,24,64]{0,2,1:T(8,128)(2,1)} reshape(bf16[8,128,1536]{1,0,2:T(8,128)(2,1)} %copy.14) | data formatting | bytes 6291456 | tf_op jit(solution)/shard_map/while/body/eval_jaxpr/cond/branch_1_fun/concatenate | solution.py:71
  348.3 6.0 %concatenate.2 = bf16[1024,24,64]{0,2,1:T(8,128)(2,1)} reshape(bf16[8,128,1536]{1,0,2:T(8,128)(2,1)} %copy.13) | data formatting | bytes 6291456 | tf_op jit(solution)/shard_map/while/body/eval_jaxpr/cond/branch_1_fun/concatenate | solution.py:72
  354.2 11.8 %bitcast_reduce_fusion = (f32[24,128]{1,0:T(8,128)S(1)}, f32[24,2048,128]{2,1,0:T(8,128)}) fusion(bf16[128,24,64]{0,2,1:T(8,128)(2,1)S(1)} %bitcast.100, bf16[1024,24,64]{0,2,1:T(8,128)(2,1)} %bitcast.96, bf16[1024,24,64]{0,2,1:T(8,128)(2,1)S(1)} %copy-done.2), kind=kOutput, calls=%fused_computation.15 | convolution fusion | flops 830469120 | bytes 31862784 | tf_op jit(solution)/shard_map/while/body/eval_jaxpr/cond/branch_1_fun/qhd,khd->hqk/dot_general | solution.py:23
  366.1 11.7 %fusion.14 = f32[24,128]{1,0:T(8,128)S(1)} fusion(f32[24,2048,128]{2,1,0:T(8,128)} %get-tuple-element.135, f32[24,128]{1,0:T(8,128)S(1)} %get-tuple-element.134), kind=kLoop, calls=%fused_computation.17 | loop fusion | flops 18871296 | bytes 25190400 | tf_op jit(solution)/shard_map/while/body/eval_jaxpr/cond/branch_1_fun/reduce_sum | solution.py:29
  377.8 11.5 %fusion.32 = bf16[128,24,64]{0,2,1:T(8,128)(2,1)S(1)} fusion(f32[24,2048,128]{2,1,0:T(8,128)} %get-tuple-element.135, f32[24,128]{1,0:T(8,128)S(1)} %get-tuple-element.134, bf16[1024,24,64]{0,2,1:T(8,128)(2,1)S(1)} %bitcast.103, bf16[1024,24,64]{0,2,1:T(8,128)(2,1)S(1)} %copy-done.4, f32[128,24]{0,1:T(8,128)S(1)} %bitcast.113), kind=kOutput, calls=%fused_computation.30 | convolution fusion | flops 837156864 | bytes 31875072 | tf_op jit(solution)/shard_map/while/body/eval_jaxpr/cond/branch_1_fun/hqk,khd->qhd/dot_general | solution.py:31
  400.7 55.2 %conditional.7 = (bf16[1,128,1536]{1,2,0:T(8,128)(2,1)S(1)}) conditional(s32[]{:T(128)} %convert_element_type.36, (bf16[128,1536]{0,1:T(8,128)(2,1)S(1)}, bf16[8,128,1536]{2,1,0:T(8,128)(2,1)}, bf16[8,128,1536]{2,1,0:T(8,128)(2,1)S(1)}) %tuple.53, (bf16[8,128,1536]{2,1,0:T(8,128)(2,1)S(1)}, bf16[1024,1536]{0,1:T(8,128)(2,1)}, ...), branch_computations={%region_1.3_spmd, %region_4.6_spmd} | conditional | flops 1686497280 | bytes 151842912
  400.7 5.0 %copy.14 = bf16[8,128,1536]{1,0,2:T(8,128)(2,1)} copy(bf16[8,128,1536]{2,1,0:T(8,128)(2,1)} %get-tuple-element.102) | data formatting | bytes 6291456 | tf_op jit(solution)/shard_map
  405.7 5.8 %concatenate.17 = bf16[1024,24,64]{0,2,1:T(8,128)(2,1)} reshape(bf16[8,128,1536]{1,0,2:T(8,128)(2,1)} %copy.14) | data formatting | bytes 6291456 | tf_op jit(solution)/shard_map/while/body/eval_jaxpr/cond/branch_1_fun/concatenate | solution.py:71
  414.9 6.0 %concatenate.2 = bf16[1024,24,64]{0,2,1:T(8,128)(2,1)} reshape(bf16[8,128,1536]{1,0,2:T(8,128)(2,1)} %copy.13) | data formatting | bytes 6291456 | tf_op jit(solution)/shard_map/while/body/eval_jaxpr/cond/branch_1_fun/concatenate | solution.py:72
  420.8 11.8 %bitcast_reduce_fusion = (f32[24,128]{1,0:T(8,128)S(1)}, f32[24,2048,128]{2,1,0:T(8,128)}) fusion(bf16[128,24,64]{0,2,1:T(8,128)(2,1)S(1)} %bitcast.100, bf16[1024,24,64]{0,2,1:T(8,128)(2,1)} %bitcast.96, bf16[1024,24,64]{0,2,1:T(8,128)(2,1)S(1)} %copy-done.2), kind=kOutput, calls=%fused_computation.15 | convolution fusion | flops 830469120 | bytes 31862784 | tf_op jit(solution)/shard_map/while/body/eval_jaxpr/cond/branch_1_fun/qhd,khd->hqk/dot_general | solution.py:23
  432.7 11.7 %fusion.14 = f32[24,128]{1,0:T(8,128)S(1)} fusion(f32[24,2048,128]{2,1,0:T(8,128)} %get-tuple-element.135, f32[24,128]{1,0:T(8,128)S(1)} %get-tuple-element.134), kind=kLoop, calls=%fused_computation.17 | loop fusion | flops 18871296 | bytes 25190400 | tf_op jit(solution)/shard_map/while/body/eval_jaxpr/cond/branch_1_fun/reduce_sum | solution.py:29
  444.4 11.5 %fusion.32 = bf16[128,24,64]{0,2,1:T(8,128)(2,1)S(1)} fusion(f32[24,2048,128]{2,1,0:T(8,128)} %get-tuple-element.135, f32[24,128]{1,0:T(8,128)S(1)} %get-tuple-element.134, bf16[1024,24,64]{0,2,1:T(8,128)(2,1)S(1)} %bitcast.103, bf16[1024,24,64]{0,2,1:T(8,128)(2,1)S(1)} %copy-done.4, f32[128,24]{0,1:T(8,128)S(1)} %bitcast.113), kind=kOutput, calls=%fused_computation.30 | convolution fusion | flops 837156864 | bytes 31875072 | tf_op jit(solution)/shard_map/while/body/eval_jaxpr/cond/branch_1_fun/hqk,khd->qhd/dot_general | solution.py:31
  (70 shorter events, 72.4 us)
Async XLA Ops:
  6.5 101.5 %copy-start.8 = (bf16[16,16,1536]{2,1,0:T(8,128)(2,1)S(1)}, bf16[16,16,1536]{2,1,0:T(8,128)(2,1)}, u32[]{:S(2)}) copy-start(bf16[16,16,1536]{2,1,0:T(8,128)(2,1)} %param.10) | copy-start | bytes 2359300
  6.5 106.4 %copy-start.7 = (bf16[16,16,1536]{2,1,0:T(8,128)(2,1)S(1)}, bf16[16,16,1536]{2,1,0:T(8,128)(2,1)}, u32[]{:S(2)}) copy-start(bf16[16,16,1536]{2,1,0:T(8,128)(2,1)} %param.11) | copy-start | bytes 2359300
  6.5 188.3 %all-gather.7.cloned.1.call-start = ((), (), s32[]{:S(2)}) async-start(), calls=%async_computation.1 | async-start | bytes 3194880 | tf_op jit(solution)/shard_map/all_gather | solution.py:55
  9.8 310.9 %all-gather.5.cloned.1.call-start = ((), (), s32[]{:S(2)}) async-start(), calls=%async_computation | async-start | bytes 3194880 | tf_op jit(solution)/shard_map/all_gather | solution.py:56
  12.4 32.5 %collective-permute-start.4 = (bf16[16,16,1536]{2,1,0:T(8,128)(2,1)}, bf16[16,16,1536]{2,1,0:T(8,128)(2,1)}, u32[]{:S(2)}, u32[]{:S(2)}) collective-permute-start(bf16[16,16,1536]{2,1,0:T(8,128)(2,1)} %param.11), channel_id=1, source_target_pairs={{0,2},{1,3},{2,4},{3,5},{4,6},{5,7},{6,8},{7,9},{8,10},{9,11},{10,... | collective-permute-start | bytes 2359304 | tf_op jit(solution)/shard_map/ppermute | solution.py:15
  15.8 65.2 %collective-permute-start = (bf16[16,16,1536]{2,1,0:T(8,128)(2,1)}, bf16[16,16,1536]{2,1,0:T(8,128)(2,1)}, u32[]{:S(2)}, u32[]{:S(2)}) collective-permute-start(bf16[16,16,1536]{2,1,0:T(8,128)(2,1)} %param.10), channel_id=1, source_target_pairs={{0,2},{1,3},{2,4},{3,5},{4,6},{5,7},{6,8},{7,9},{8,10},{9,11},{10,... | collective-permute-start | bytes 2359304 | tf_op jit(solution)/shard_map/ppermute | solution.py:15
  20.2 87.8 %collective-permute-start.5 = (bf16[16,16,1536]{2,1,0:T(8,128)(2,1)}, bf16[16,16,1536]{2,1,0:T(8,128)(2,1)}, u32[]{:S(2)}, u32[]{:S(2)}) collective-permute-start(bf16[16,16,1536]{2,1,0:T(8,128)(2,1)} %param.11), channel_id=1, source_target_pairs={{0,1},{1,2},{2,3},{3,4},{4,5},{5,6},{6,7},{7,8},{8,9},{9,10},{10,1... | collective-permute-start | bytes 2359304 | tf_op jit(solution)/shard_map/ppermute | solution.py:15
  21.3 130.3 %collective-permute-start.2 = (bf16[16,16,1536]{2,1,0:T(8,128)(2,1)}, bf16[16,16,1536]{2,1,0:T(8,128)(2,1)S(1)}, u32[]{:S(2)}, u32[]{:S(2)}) collective-permute-start(bf16[16,16,1536]{2,1,0:T(8,128)(2,1)} %param.10), channel_id=1, source_target_pairs={{0,63},{1,0},{2,1},{3,2},{4,3},{5,4},{6,5},{7,6},{8,7},{9,8},{10,9... | collective-permute-start | bytes 2359304 | tf_op jit(solution)/shard_map/ppermute | solution.py:15
  24.4 125.2 %collective-permute-start.1 = (bf16[16,16,1536]{2,1,0:T(8,128)(2,1)}, bf16[16,16,1536]{2,1,0:T(8,128)(2,1)S(1)}, u32[]{:S(2)}, u32[]{:S(2)}) collective-permute-start(bf16[16,16,1536]{2,1,0:T(8,128)(2,1)} %param.10), channel_id=1, source_target_pairs={{0,1},{1,2},{2,3},{3,4},{4,5},{5,6},{6,7},{7,8},{8,9},{9,10},{10,1... | collective-permute-start | bytes 2359304 | tf_op jit(solution)/shard_map/ppermute | solution.py:15
  44.9 68.9 %collective-permute-start.6 = (bf16[16,16,1536]{2,1,0:T(8,128)(2,1)}, bf16[16,16,1536]{2,1,0:T(8,128)(2,1)S(1)}, u32[]{:S(2)}, u32[]{:S(2)}) collective-permute-start(bf16[16,16,1536]{2,1,0:T(8,128)(2,1)} %param.11), channel_id=1, source_target_pairs={{0,63},{1,0},{2,1},{3,2},{4,3},{5,4},{6,5},{7,6},{8,7},{9,8},{10,9... | collective-permute-start | bytes 2359304 | tf_op jit(solution)/shard_map/ppermute | solution.py:15
  80.9 67.7 %collective-permute-start.7 = (bf16[16,16,1536]{2,1,0:T(8,128)(2,1)}, bf16[16,16,1536]{2,1,0:T(8,128)(2,1)S(1)}, u32[]{:S(2)}, u32[]{:S(2)}) collective-permute-start(bf16[16,16,1536]{2,1,0:T(8,128)(2,1)} %param.11), channel_id=1, source_target_pairs={{0,62},{1,63},{2,0},{3,1},{4,2},{5,3},{6,4},{7,5},{8,6},{9,7},{10,... | collective-permute-start | bytes 2359304 | tf_op jit(solution)/shard_map/ppermute | solution.py:15
  108.0 59.4 %collective-permute-start.3 = (bf16[16,16,1536]{2,1,0:T(8,128)(2,1)S(1)}, bf16[16,16,1536]{2,1,0:T(8,128)(2,1)S(1)}, u32[]{:S(2)}, u32[]{:S(2)}) collective-permute-start(bf16[16,16,1536]{2,1,0:T(8,128)(2,1)S(1)} %copy-done.8), channel_id=1, source_target_pairs={{0,62},{1,63},{2,0},{3,1},{4,2},{5,3},{6,4},{7,5},{8,6},{9,7},{10,... | collective-permute-start | bytes 2359304 | tf_op jit(solution)/shard_map/ppermute | solution.py:15
  199.5 125.8 %copy-start.9 = (s32[2,1,8]{2,1,0:T(1,128)S(1)}, s32[2,1,8]{2,1,0:T(1,128)}, u32[]{:S(2)}) copy-start(s32[2,1,8]{2,1,0:T(1,128)} %param.12) | copy-start | bytes 196
  348.2 6.0 %copy-start.2 = (bf16[1024,24,64]{0,2,1:T(8,128)(2,1)S(1)}, bf16[1024,24,64]{0,2,1:T(8,128)(2,1)}, u32[]{:S(2)}) copy-start(bf16[1024,24,64]{0,2,1:T(8,128)(2,1)} %concatenate.17) | copy-start | bytes 9437188 | tf_op jit(solution)/shard_map/conditional.1
  366.1 11.7 %copy-start.4 = (bf16[1024,24,64]{0,2,1:T(8,128)(2,1)S(1)}, bf16[1024,24,64]{0,2,1:T(8,128)(2,1)}, u32[]{:S(2)}) copy-start(bf16[1024,24,64]{0,2,1:T(8,128)(2,1)} %concatenate.2) | copy-start | bytes 9437188 | tf_op jit(solution)/shard_map/conditional.1
  366.1 11.7 %copy-start.6 = (bf16[1024,1536]{0,1:T(8,128)(2,1)S(1)}, bf16[1024,1536]{0,1:T(8,128)(2,1)}, u32[]{:S(2)}) copy-start(bf16[1024,1536]{0,1:T(8,128)(2,1)} %get-tuple-element.72) | copy-start | bytes 9437188 | tf_op jit(solution)/shard_map/conditional.1
  389.3 0.8 copy-start.5
  414.9 6.0 %copy-start.2 = (bf16[1024,24,64]{0,2,1:T(8,128)(2,1)S(1)}, bf16[1024,24,64]{0,2,1:T(8,128)(2,1)}, u32[]{:S(2)}) copy-start(bf16[1024,24,64]{0,2,1:T(8,128)(2,1)} %concatenate.17) | copy-start | bytes 9437188 | tf_op jit(solution)/shard_map/conditional.1
  432.7 11.7 %copy-start.4 = (bf16[1024,24,64]{0,2,1:T(8,128)(2,1)S(1)}, bf16[1024,24,64]{0,2,1:T(8,128)(2,1)}, u32[]{:S(2)}) copy-start(bf16[1024,24,64]{0,2,1:T(8,128)(2,1)} %concatenate.2) | copy-start | bytes 9437188 | tf_op jit(solution)/shard_map/conditional.1
  432.7 11.7 %copy-start.6 = (bf16[1024,1536]{0,1:T(8,128)(2,1)S(1)}, bf16[1024,1536]{0,1:T(8,128)(2,1)}, u32[]{:S(2)}) copy-start(bf16[1024,1536]{0,1:T(8,128)(2,1)} %get-tuple-element.72) | copy-start | bytes 9437188 | tf_op jit(solution)/shard_map/conditional.1
  455.9 0.8 copy-start.5
Sparse Core Ops, SparseCore 0:
  11.0 183.7 all-gather.6
  198.5 122.1 all-gather.4
where the time goes:
time: 467 us; the launch traced here: 465 us
  waiting for transfers between devices  235 us (50%)
  local copies, waits for them, and re-layouts  90.3 us (19%)
  starting transfers between devices  55.8 us (12%)
  matrix products  46.7 us (10%)
  other arithmetic  24.1 us (5%)
  between operations  13.4 us (3%)
    all_gather x1, waiting for transfers between devices, local(): lax.all_gather(picked_values, 'lon', axis=0, tiled=True)  121 us
    ppermute x8, waiting for transfers between devices, from_behind(): return lax.ppermute(value, axis, pairs)  87.2 us
    ppermute x8, starting transfers between devices, from_behind(): return lax.ppermute(value, axis, pairs)  55.7 us
    all_gather x1, waiting for transfers between devices, local(): lax.all_gather(picked_keys, 'lon', axis=0, tiled=True)  26.5 us
    dot_general x2, matrix products, block_attention(): jnp.einsum('qhd,khd->hqk', q_heads, k_heads, preferred_element_type=jnp.f...  23.7 us
    reduce_sum x2, other arithmetic, block_attention(): totals = jnp.sum(exp_scores, axis=-1)  23.3 us
    dot_general x2, matrix products, block_attention(): jnp.einsum('hqk,khd->qhd', weights, v_heads, preferred_element_type=jnp.f...  23 us
    another operation x16, local copies, waits for them, and re-layouts  16.8 us
  transfers between devices with their start and end apart: 10, of which 7 were waited for; matrix products, arithmetic and copies ran while one was open for 4% of the time, Pallas kernels for 0%

commit v1 on v0

--- a/solution.py
+++ b/solution.py
@@ -7,6 +7,13 @@
 HD = 64
 BR = 8
 BW = 16
+
+
+def all_by_exchange(x, mesh_axis, d):
+    peers = lax.axis_size(mesh_axis)
+    shards = jnp.stack([x for _ in range(peers)])
+    shards = lax.all_to_all(shards, mesh_axis, split_axis=0, concat_axis=0)
+    return jnp.concatenate(shards, axis=d)
 
 
 def from_behind(value, axis, steps):
@@ -53,7 +60,7 @@
     picked_values = value_tokens.reshape(tile_lat * tile_lon, feature)[band_rows[0]]
     band_keys, band_values = (
         lax.all_gather(picked_keys, "lon", axis=0, tiled=True),
-        lax.all_gather(picked_values, "lon", axis=0, tiled=True),
+        all_by_exchange(picked_values, "lon", 0),
     )
     lat_at = lax.axis_index("lat")
     is_polar = (lat_at == 0) | (lat_at == lat_size - 1)

time: 467 us -> 396 us (0.85)
  waiting for transfers between devices: 235 us -> 164 us
  starting transfers between devices: 55.8 us -> 49.6 us
    all_gather x1 -> x0, waiting for transfers between devices: 121 us -> none  [local(): lax.all_gather(picked_values, 'lon', axis=0, tiled=True)]
    ppermute x8, waiting for transfers between devices: 87.2 us -> 164 us  [from_behind(): return lax.ppermute(value, axis, pairs)]
    all_gather x1, waiting for transfers between devices: 26.5 us -> 0.01 us  [local(): lax.all_gather(picked_keys, 'lon', axis=0, tiled=True)]
    ppermute x8, starting transfers between devices: 55.7 us -> 35 us  [from_behind(): return lax.ppermute(value, axis, pairs)]
    all_to_all x0 -> x1, starting transfers between devices: none -> 14.6 us  [all_by_exchange(): shards = lax.all_to_all(shards, mesh_axis, split_axis=0, concat_axis=0)]
    another operation x16 -> x17, local copies, waits for them, and re-layouts: 16.8 us -> 18.9 us
  transfers between devices with their start and end apart: 10 -> 10, of which waited for: 7 -> 5; matrix products, arithmetic and copies ran while one was open for 4% -> 5% of each run, Pallas kernels for 0% -> 0%
where the time goes in v1:
time: 396 us; the launch traced here: 390 us
  waiting for transfers between devices  164 us (41%)
  local copies, waits for them, and re-layouts  92.3 us (23%)
  starting transfers between devices  49.6 us (13%)
  matrix products  46.7 us (12%)
  other arithmetic  24 us (6%)
  between operations  13.4 us (3%)
    ppermute x8, waiting for transfers between devices, from_behind(): return lax.ppermute(value, axis, pairs)  164 us
    ppermute x8, starting transfers between devices, from_behind(): return lax.ppermute(value, axis, pairs)  35 us
    dot_general x2, matrix products, block_attention(): jnp.einsum('qhd,khd->hqk', q_heads, k_heads, preferred_element_type=jnp.f...  23.7 us
    reduce_sum x2, other arithmetic, block_attention(): totals = jnp.sum(exp_scores, axis=-1)  23.3 us
    dot_general x2, matrix products, block_attention(): jnp.einsum('hqk,khd->qhd', weights, v_heads, preferred_element_type=jnp.f...  23 us
    another operation x16, local copies, waits for them, and re-layouts  16.8 us
    all_to_all x1, starting transfers between devices, all_by_exchange(): shards = lax.all_to_all(shards, mesh_axis, split_axis=0, concat_axis=0)  14.6 us
    unnamed x14, local copies, waits for them, and re-layouts  13.4 us
  transfers between devices with their start and end apart: 10, of which 5 were waited for; matrix products, arithmetic and copies ran while one was open for 5% of the time, Pallas kernels for 0%

profile of v1, /device:TPU:8, one launch (start us, length us, event | category | flops | bytes accessed | tf_op | source)
XLA Modules:
  0.0 390.4 jit_solution(7236557583487858519)
XLA Ops:
  11.1 14.6 %all-to-all-start = ((bf16[64,16,1536]{2,1,0:T(8,128)(2,1)}), bf16[64,16,1536]{2,1,0:T(8,128)(2,1)S(1)}, u32[]{:S(2)}, u32[]{:S(2)}) async-start(bf16[64,16,1536]{2,1,0:T(8,128)(2,1)} %stack.2), calls=%async_computation | async-start | bytes 6291456 | tf_op jit(solution)/shard_map/all_to_all | solution.py:15
  38.4 94.1 %collective-permute-done.4 = bf16[16,16,1536]{2,1,0:T(8,128)(2,1)} collective-permute-done((bf16[16,16,1536]{2,1,0:T(8,128)(2,1)}, bf16[16,16,1536]{2,1,0:T(8,128)(2,1)}, u32[]{:S(2)}, u32[]{:S(2)}) %collective-permute-start.4) | collective-permute-done | bytes 786464 | tf_op jit(solution)/shard_map/ppermute | solution.py:22
  132.5 19.5 %collective-permute-start.6 = (bf16[16,16,1536]{2,1,0:T(8,128)(2,1)}, bf16[16,16,1536]{2,1,0:T(8,128)(2,1)S(1)}, u32[]{:S(2)}, u32[]{:S(2)}) collective-permute-start(bf16[16,16,1536]{2,1,0:T(8,128)(2,1)} %param.11), channel_id=1, source_target_pairs={{0,63},{1,0},{2,1},{3,2},{4,3},{5,4},{6,5},{7,6},{8,7},{9,8},{10,9... | collective-permute-start | bytes 2359304 | tf_op jit(solution)/shard_map/ppermute | solution.py:22
  154.1 26.2 %collective-permute-done = bf16[16,16,1536]{2,1,0:T(8,128)(2,1)} collective-permute-done((bf16[16,16,1536]{2,1,0:T(8,128)(2,1)}, bf16[16,16,1536]{2,1,0:T(8,128)(2,1)}, u32[]{:S(2)}, u32[]{:S(2)}) %collective-permute-start) | collective-permute-done | bytes 786464 | tf_op jit(solution)/shard_map/ppermute | solution.py:22
  185.4 11.8 %collective-permute-done.5 = bf16[16,16,1536]{2,1,0:T(8,128)(2,1)} collective-permute-done((bf16[16,16,1536]{2,1,0:T(8,128)(2,1)}, bf16[16,16,1536]{2,1,0:T(8,128)(2,1)}, u32[]{:S(2)}, u32[]{:S(2)}) %collective-permute-start.5) | collective-permute-done | bytes 786464 | tf_op jit(solution)/shard_map/ppermute | solution.py:22
  203.6 29.6 %collective-permute-done.7 = bf16[16,16,1536]{2,1,0:T(8,128)(2,1)S(1)} collective-permute-done((bf16[16,16,1536]{2,1,0:T(8,128)(2,1)}, bf16[16,16,1536]{2,1,0:T(8,128)(2,1)S(1)}, u32[]{:S(2)}, u32[]{:S(2)}) %collective-permute-start.7) | collective-permute-done | bytes 786464 | tf_op jit(solution)/shard_map/ppermute | solution.py:22
  245.7 4.6 %copy.17 = bf16[1024,1536]{0,1:T(8,128)(2,1)} copy(bf16[1024,1536]{1,0:T(8,128)(2,1)} %all-gather.3.cloned.1.call-done) | data formatting | bytes 6291456 | tf_op jit(solution)/shard_map/while | solution.py:88
  250.3 133.3 %while.10 = (s32[]{:T(128)}, bf16[2,128,1536]{2,1,0:T(8,128)(2,1)}, pred[]{:T(512)}, bf16[2,128,1536]{2,1,0:T(8,128)(2,1)}, s32[2,8]{1,0:T(2,128)S(1)}, /*index=...) while((s32[]{:T(128)}, bf16[2,128,1536]{2,1,0:T(8,128)(2,1)}, ...), condition=%wide.region_7.8_spmd, body=%wide.region_0.7_spmd.sunk | while | flops 1686498304 | bytes 169148896 | solution.py:88
  254.5 4.5 %gather_fusion = bf16[8,128,1536]{2,1,0:T(8,128)(2,1)} fusion(bf16[10,128,1536]{2,1,0:T(8,128)(2,1)} %get-tuple-element.216, s32[1024]{0:T(1024)S(1)} %pad_clamp_fusion.3), kind=kCustom, calls=%fused_computation.clone.1 | custom fusion | bytes 6291488 | tf_op jit(solution)/shard_map/while/body/eval_jaxpr/gather | solution.py:73
  259.0 55.2 %conditional.7 = (bf16[1,128,1536]{1,2,0:T(8,128)(2,1)S(1)}) conditional(s32[]{:T(128)} %convert_element_type.36, (bf16[128,1536]{0,1:T(8,128)(2,1)S(1)}, bf16[8,128,1536]{2,1,0:T(8,128)(2,1)}, bf16[8,128,1536]{2,1,0:T(8,128)(2,1)S(1)}) %tuple.51, (bf16[8,128,1536]{2,1,0:T(8,128)(2,1)S(1)}, bf16[1024,1536]{0,1:T(8,128)(2,1)}, ...), branch_computations={%region_1.3_spmd, %region_4.6_spmd} | conditional | flops 1686497280 | bytes 151842912
  259.0 5.0 %copy.14 = bf16[8,128,1536]{1,0,2:T(8,128)(2,1)} copy(bf16[8,128,1536]{2,1,0:T(8,128)(2,1)} %get-tuple-element.102) | data formatting | bytes 6291456 | tf_op jit(solution)/shard_map
  264.0 5.8 %concatenate.17 = bf16[1024,24,64]{0,2,1:T(8,128)(2,1)} reshape(bf16[8,128,1536]{1,0,2:T(8,128)(2,1)} %copy.14) | data formatting | bytes 6291456 | tf_op jit(solution)/shard_map/while/body/eval_jaxpr/cond/branch_1_fun/concatenate | solution.py:78
  273.2 6.0 %concatenate.2 = bf16[1024,24,64]{0,2,1:T(8,128)(2,1)} reshape(bf16[8,128,1536]{1,0,2:T(8,128)(2,1)} %copy.13) | data formatting | bytes 6291456 | tf_op jit(solution)/shard_map/while/body/eval_jaxpr/cond/branch_1_fun/concatenate | solution.py:79
  279.2 11.8 %bitcast_reduce_fusion = (f32[24,128]{1,0:T(8,128)S(1)}, f32[24,2048,128]{2,1,0:T(8,128)}) fusion(bf16[128,24,64]{0,2,1:T(8,128)(2,1)S(1)} %bitcast.101, bf16[1024,24,64]{0,2,1:T(8,128)(2,1)} %bitcast.97, bf16[1024,24,64]{0,2,1:T(8,128)(2,1)S(1)} %copy-done.2), kind=kOutput, calls=%fused_computation.15 | convolution fusion | flops 830469120 | bytes 31862784 | tf_op jit(solution)/shard_map/while/body/eval_jaxpr/cond/branch_1_fun/qhd,khd->hqk/dot_general | solution.py:30
  291.0 11.7 %fusion.14 = f32[24,128]{1,0:T(8,128)S(1)} fusion(f32[24,2048,128]{2,1,0:T(8,128)} %get-tuple-element.135, f32[24,128]{1,0:T(8,128)S(1)} %get-tuple-element.134), kind=kLoop, calls=%fused_computation.17 | loop fusion | flops 18871296 | bytes 25190400 | tf_op jit(solution)/shard_map/while/body/eval_jaxpr/cond/branch_1_fun/reduce_sum | solution.py:36
  302.7 11.5 %fusion.32 = bf16[128,24,64]{0,2,1:T(8,128)(2,1)S(1)} fusion(f32[24,2048,128]{2,1,0:T(8,128)} %get-tuple-element.135, f32[24,128]{1,0:T(8,128)S(1)} %get-tuple-element.134, bf16[1024,24,64]{0,2,1:T(8,128)(2,1)S(1)} %bitcast.105, bf16[1024,24,64]{0,2,1:T(8,128)(2,1)S(1)} %copy-done.4, f32[128,24]{0,1:T(8,128)S(1)} %bitcast.113), kind=kOutput, calls=%fused_computation.30 | convolution fusion | flops 837156864 | bytes 31875072 | tf_op jit(solution)/shard_map/while/body/eval_jaxpr/cond/branch_1_fun/hqk,khd->qhd/dot_general | solution.py:38
  321.1 4.5 %gather_fusion = bf16[8,128,1536]{2,1,0:T(8,128)(2,1)} fusion(bf16[10,128,1536]{2,1,0:T(8,128)(2,1)} %get-tuple-element.216, s32[1024]{0:T(1024)S(1)} %pad_clamp_fusion.3), kind=kCustom, calls=%fused_computation.clone.1 | custom fusion | bytes 6291488 | tf_op jit(solution)/shard_map/while/body/eval_jaxpr/gather | solution.py:73
  325.6 55.2 %conditional.7 = (bf16[1,128,1536]{1,2,0:T(8,128)(2,1)S(1)}) conditional(s32[]{:T(128)} %convert_element_type.36, (bf16[128,1536]{0,1:T(8,128)(2,1)S(1)}, bf16[8,128,1536]{2,1,0:T(8,128)(2,1)}, bf16[8,128,1536]{2,1,0:T(8,128)(2,1)S(1)}) %tuple.51, (bf16[8,128,1536]{2,1,0:T(8,128)(2,1)S(1)}, bf16[1024,1536]{0,1:T(8,128)(2,1)}, ...), branch_computations={%region_1.3_spmd, %region_4.6_spmd} | conditional | flops 1686497280 | bytes 151842912
  325.6 5.0 %copy.14 = bf16[8,128,1536]{1,0,2:T(8,128)(2,1)} copy(bf16[8,128,1536]{2,1,0:T(8,128)(2,1)} %get-tuple-element.102) | data formatting | bytes 6291456 | tf_op jit(solution)/shard_map
  330.6 5.8 %concatenate.17 = bf16[1024,24,64]{0,2,1:T(8,128)(2,1)} reshape(bf16[8,128,1536]{1,0,2:T(8,128)(2,1)} %copy.14) | data formatting | bytes 6291456 | tf_op jit(solution)/shard_map/while/body/eval_jaxpr/cond/branch_1_fun/concatenate | solution.py:78
  339.8 6.0 %concatenate.2 = bf16[1024,24,64]{0,2,1:T(8,128)(2,1)} reshape(bf16[8,128,1536]{1,0,2:T(8,128)(2,1)} %copy.13) | data formatting | bytes 6291456 | tf_op jit(solution)/shard_map/while/body/eval_jaxpr/cond/branch_1_fun/concatenate | solution.py:79
  345.8 11.8 %bitcast_reduce_fusion = (f32[24,128]{1,0:T(8,128)S(1)}, f32[24,2048,128]{2,1,0:T(8,128)}) fusion(bf16[128,24,64]{0,2,1:T(8,128)(2,1)S(1)} %bitcast.101, bf16[1024,24,64]{0,2,1:T(8,128)(2,1)} %bitcast.97, bf16[1024,24,64]{0,2,1:T(8,128)(2,1)S(1)} %copy-done.2), kind=kOutput, calls=%fused_computation.15 | convolution fusion | flops 830469120 | bytes 31862784 | tf_op jit(solution)/shard_map/while/body/eval_jaxpr/cond/branch_1_fun/qhd,khd->hqk/dot_general | solution.py:30
  357.7 11.7 %fusion.14 = f32[24,128]{1,0:T(8,128)S(1)} fusion(f32[24,2048,128]{2,1,0:T(8,128)} %get-tuple-element.135, f32[24,128]{1,0:T(8,128)S(1)} %get-tuple-element.134), kind=kLoop, calls=%fused_computation.17 | loop fusion | flops 18871296 | bytes 25190400 | tf_op jit(solution)/shard_map/while/body/eval_jaxpr/cond/branch_1_fun/reduce_sum | solution.py:36
  369.4 11.5 %fusion.32 = bf16[128,24,64]{0,2,1:T(8,128)(2,1)S(1)} fusion(f32[24,2048,128]{2,1,0:T(8,128)} %get-tuple-element.135, f32[24,128]{1,0:T(8,128)S(1)} %get-tuple-element.134, bf16[1024,24,64]{0,2,1:T(8,128)(2,1)S(1)} %bitcast.105, bf16[1024,24,64]{0,2,1:T(8,128)(2,1)S(1)} %copy-done.4, f32[128,24]{0,1:T(8,128)S(1)} %bitcast.113), kind=kOutput, calls=%fused_computation.30 | convolution fusion | flops 837156864 | bytes 31875072 | tf_op jit(solution)/shard_map/while/body/eval_jaxpr/cond/branch_1_fun/hqk,khd->qhd/dot_general | solution.py:38
  (70 shorter events, 63.9 us)
Async XLA Ops:
  11.1 231.6 %all-to-all-start = ((bf16[64,16,1536]{2,1,0:T(8,128)(2,1)}), bf16[64,16,1536]{2,1,0:T(8,128)(2,1)S(1)}, u32[]{:S(2)}, u32[]{:S(2)}) async-start(bf16[64,16,1536]{2,1,0:T(8,128)(2,1)} %stack.2), calls=%async_computation | async-start | bytes 6291456 | tf_op jit(solution)/shard_map/all_to_all | solution.py:15
  25.7 219.9 %all-gather.3.cloned.1.call-start = ((), (), s32[]{:S(2)}) async-start(), calls=%async_computation.1 | async-start | bytes 3194880 | tf_op jit(solution)/shard_map/all_gather | solution.py:62
  28.3 104.2 %collective-permute-start.4 = (bf16[16,16,1536]{2,1,0:T(8,128)(2,1)}, bf16[16,16,1536]{2,1,0:T(8,128)(2,1)}, u32[]{:S(2)}, u32[]{:S(2)}) collective-permute-start(bf16[16,16,1536]{2,1,0:T(8,128)(2,1)} %param.11), channel_id=1, source_target_pairs={{0,2},{1,3},{2,4},{3,5},{4,6},{5,7},{6,8},{7,9},{8,10},{9,11},{10,... | collective-permute-start | bytes 2359304 | tf_op jit(solution)/shard_map/ppermute | solution.py:22
  30.7 149.6 %collective-permute-start = (bf16[16,16,1536]{2,1,0:T(8,128)(2,1)}, bf16[16,16,1536]{2,1,0:T(8,128)(2,1)}, u32[]{:S(2)}, u32[]{:S(2)}) collective-permute-start(bf16[16,16,1536]{2,1,0:T(8,128)(2,1)} %param.10), channel_id=1, source_target_pairs={{0,2},{1,3},{2,4},{3,5},{4,6},{5,7},{6,8},{7,9},{8,10},{9,11},{10,... | collective-permute-start | bytes 2359304 | tf_op jit(solution)/shard_map/ppermute | solution.py:22
  34.3 162.9 %collective-permute-start.5 = (bf16[16,16,1536]{2,1,0:T(8,128)(2,1)}, bf16[16,16,1536]{2,1,0:T(8,128)(2,1)}, u32[]{:S(2)}, u32[]{:S(2)}) collective-permute-start(bf16[16,16,1536]{2,1,0:T(8,128)(2,1)} %param.11), channel_id=1, source_target_pairs={{0,1},{1,2},{2,3},{3,4},{4,5},{5,6},{6,7},{7,8},{8,9},{9,10},{10,1... | collective-permute-start | bytes 2359304 | tf_op jit(solution)/shard_map/ppermute | solution.py:22
  34.9 202.3 %collective-permute-start.2 = (bf16[16,16,1536]{2,1,0:T(8,128)(2,1)}, bf16[16,16,1536]{2,1,0:T(8,128)(2,1)}, u32[]{:S(2)}, u32[]{:S(2)}) collective-permute-start(bf16[16,16,1536]{2,1,0:T(8,128)(2,1)} %param.10), channel_id=1, source_target_pairs={{0,63},{1,0},{2,1},{3,2},{4,3},{5,4},{6,5},{7,6},{8,7},{9,8},{10,9... | collective-permute-start | bytes 2359304 | tf_op jit(solution)/shard_map/ppermute | solution.py:22
  38.4 195.7 %collective-permute-start.1 = (bf16[16,16,1536]{2,1,0:T(8,128)(2,1)}, bf16[16,16,1536]{2,1,0:T(8,128)(2,1)}, u32[]{:S(2)}, u32[]{:S(2)}) collective-permute-start(bf16[16,16,1536]{2,1,0:T(8,128)(2,1)} %param.10), channel_id=1, source_target_pairs={{0,1},{1,2},{2,3},{3,4},{4,5},{5,6},{6,7},{7,8},{8,9},{9,10},{10,1... | collective-permute-start | bytes 2359304 | tf_op jit(solution)/shard_map/ppermute | solution.py:22
  38.4 163.3 %copy-start.7 = (bf16[16,16,1536]{2,1,0:T(8,128)(2,1)S(1)}, bf16[16,16,1536]{2,1,0:T(8,128)(2,1)}, u32[]{:S(2)}) copy-start(bf16[16,16,1536]{2,1,0:T(8,128)(2,1)} %param.11) | copy-start | bytes 2359300
  132.5 70.1 %collective-permute-start.6 = (bf16[16,16,1536]{2,1,0:T(8,128)(2,1)}, bf16[16,16,1536]{2,1,0:T(8,128)(2,1)S(1)}, u32[]{:S(2)}, u32[]{:S(2)}) collective-permute-start(bf16[16,16,1536]{2,1,0:T(8,128)(2,1)} %param.11), channel_id=1, source_target_pairs={{0,63},{1,0},{2,1},{3,2},{4,3},{5,4},{6,5},{7,6},{8,7},{9,8},{10,9... | collective-permute-start | bytes 2359304 | tf_op jit(solution)/shard_map/ppermute | solution.py:22
  180.3 52.9 %collective-permute-start.7 = (bf16[16,16,1536]{2,1,0:T(8,128)(2,1)}, bf16[16,16,1536]{2,1,0:T(8,128)(2,1)S(1)}, u32[]{:S(2)}, u32[]{:S(2)}) collective-permute-start(bf16[16,16,1536]{2,1,0:T(8,128)(2,1)} %param.11), channel_id=1, source_target_pairs={{0,62},{1,63},{2,0},{3,1},{4,2},{5,3},{6,4},{7,5},{8,6},{9,7},{10,... | collective-permute-start | bytes 2359304 | tf_op jit(solution)/shard_map/ppermute | solution.py:22
  197.2 44.7 %collective-permute-start.3 = (bf16[16,16,1536]{2,1,0:T(8,128)(2,1)}, bf16[16,16,1536]{2,1,0:T(8,128)(2,1)S(1)}, u32[]{:S(2)}, u32[]{:S(2)}) collective-permute-start(bf16[16,16,1536]{2,1,0:T(8,128)(2,1)} %param.10), channel_id=1, source_target_pairs={{0,62},{1,63},{2,0},{3,1},{4,2},{5,3},{6,4},{7,5},{8,6},{9,7},{10,... | collective-permute-start | bytes 2359304 | tf_op jit(solution)/shard_map/ppermute | solution.py:22
  199.6 36.6 %copy-start.8 = (bf16[16,16,1536]{2,1,0:T(8,128)(2,1)S(1)}, bf16[16,16,1536]{2,1,0:T(8,128)(2,1)}, u32[]{:S(2)}) copy-start(bf16[16,16,1536]{2,1,0:T(8,128)(2,1)} %param.10) | copy-start | bytes 2359300
  245.7 4.6 %copy-start.9 = (s32[2,1,8]{2,1,0:T(1,128)S(1)}, s32[2,1,8]{2,1,0:T(1,128)}, u32[]{:S(2)}) copy-start(s32[2,1,8]{2,1,0:T(1,128)} %param.12) | copy-start | bytes 196
  273.2 6.0 %copy-start.2 = (bf16[1024,24,64]{0,2,1:T(8,128)(2,1)S(1)}, bf16[1024,24,64]{0,2,1:T(8,128)(2,1)}, u32[]{:S(2)}) copy-start(bf16[1024,24,64]{0,2,1:T(8,128)(2,1)} %concatenate.17) | copy-start | bytes 9437188 | tf_op jit(solution)/shard_map/conditional.1
  291.0 11.7 %copy-start.4 = (bf16[1024,24,64]{0,2,1:T(8,128)(2,1)S(1)}, bf16[1024,24,64]{0,2,1:T(8,128)(2,1)}, u32[]{:S(2)}) copy-start(bf16[1024,24,64]{0,2,1:T(8,128)(2,1)} %concatenate.2) | copy-start | bytes 9437188 | tf_op jit(solution)/shard_map/conditional.1
  291.0 11.7 %copy-start.6 = (bf16[1024,1536]{0,1:T(8,128)(2,1)S(1)}, bf16[1024,1536]{0,1:T(8,128)(2,1)}, u32[]{:S(2)}) copy-start(bf16[1024,1536]{0,1:T(8,128)(2,1)} %get-tuple-element.72) | copy-start | bytes 9437188 | tf_op jit(solution)/shard_map/conditional.1
  314.2 0.8 copy-start.5
  339.8 6.0 %copy-start.2 = (bf16[1024,24,64]{0,2,1:T(8,128)(2,1)S(1)}, bf16[1024,24,64]{0,2,1:T(8,128)(2,1)}, u32[]{:S(2)}) copy-start(bf16[1024,24,64]{0,2,1:T(8,128)(2,1)} %concatenate.17) | copy-start | bytes 9437188 | tf_op jit(solution)/shard_map/conditional.1
  357.7 11.7 %copy-start.4 = (bf16[1024,24,64]{0,2,1:T(8,128)(2,1)S(1)}, bf16[1024,24,64]{0,2,1:T(8,128)(2,1)}, u32[]{:S(2)}) copy-start(bf16[1024,24,64]{0,2,1:T(8,128)(2,1)} %concatenate.2) | copy-start | bytes 9437188 | tf_op jit(solution)/shard_map/conditional.1
  357.7 11.7 %copy-start.6 = (bf16[1024,1536]{0,1:T(8,128)(2,1)S(1)}, bf16[1024,1536]{0,1:T(8,128)(2,1)}, u32[]{:S(2)}) copy-start(bf16[1024,1536]{0,1:T(8,128)(2,1)} %get-tuple-element.72) | copy-start | bytes 9437188 | tf_op jit(solution)/shard_map/conditional.1
  380.9 0.8 copy-start.5
Sparse Core Ops, SparseCore 0:
  30.2 141.0 all-gather.2
